TPU v7x, 512 devices: a whole 4x8x8 slice. The times are simulated.
512 devices in a mesh: ctx: 64 (over z_hi, y, core), tp: 8 (over x, z_lo).
Axes of the slice: x: 4, y: 8, z: 8 (z_hi: 4, z_lo: 2; z = z_hi * 2 + z_lo), core: 2. Of those that a mesh axis runs over, the one named last changes fastest.
Arguments:
- query_in: bfloat16 [1024, 16384], P('tp', 'ctx'), may hold values from -6 to 6
- key_in: bfloat16 [1024, 16384], P('tp', 'ctx'), may hold values from -6 to 6
- value_in: bfloat16 [1024, 16384], P('tp', 'ctx'), may hold values from -6 to 6
- short_kernel: float32 [3, 1024, 7], P(None, 'tp'), may hold values from -2 to 2
- basis_weight: float32 [64, 33], replicated, may hold values from -96 to 96
- basis_bias: float32 [64], replicated, may hold values from -3.140625 to 3.140625
- filter_proj: float32 [1024, 64], P('tp'), may hold values from -0.75 to 0.75
- decay_rate: float32 [1024], P('tp'), as said below
- skip_gain: float32 [1024], P('tp'), may hold values from -3 to 3
- grad_out: bfloat16 [1024, 16384], P('tp', 'ctx'), may hold values from -6 to 6
Outputs:
- mixed: bfloat16 [1024, 16384], P('tp', 'ctx')
- grad_query: bfloat16 [1024, 16384], P('tp', 'ctx')
- grad_key: bfloat16 [1024, 16384], P('tp', 'ctx')
- grad_value: bfloat16 [1024, 16384], P('tp', 'ctx')
- grad_proj: float32 [1024, 64], P('tp')
- grad_basis: float32 [64, 33], replicated
Inputs may be any that keep to these rules, and one draw needn't show every extreme that they name: decay_rate is positive in every channel.
All inputs are finite; a program needn't handle non-finite values.
Results may differ from a plain program's by a relative error of at most 0.0066.
Values may be sent and summed in bfloat16 or wider, within the bound.
No kernel may reach another device: no remote copies, remote signals or barrier semaphores. Data moves between devices by JAX's collectives and lax.ppermute only.
A program may use at most 64 MiB of HBM per device.

v0:
```python
import math
import jax
import jax.numpy as jnp
from jax import lax
from jax.sharding import PartitionSpec as P

PRECISE = lax.Precision.HIGHEST


def passed_along(value, axis, steps):
    count = lax.axis_size(axis)
    leading, last = (max(0, -steps), min(count, count - steps))
    return lax.ppermute(value, axis, [(source, source + steps) for source in range(leading, last)])


def features(offset_pos, num_pos, seq_total, num_freq):
    positions = offset_pos + jnp.arange(num_pos, dtype=jnp.int32)
    pieces = [positions.astype(jnp.float32) / seq_total]
    for harmonic in range(1, num_freq + 1):
        angles = (harmonic * positions % seq_total).astype(jnp.float32) * (
            2.0 * math.pi / seq_total
        )
        pieces.append(jnp.cos(angles))
        pieces.append(jnp.sin(angles))
    return jnp.stack(pieces)


def window(decay_rate, offset_pos, num_pos, seq_total):
    positions = (offset_pos + jnp.arange(num_pos, dtype=jnp.int32)).astype(jnp.float32)
    energy = jnp.expm1(-2.0 * decay_rate) / jnp.expm1(-2.0 * decay_rate / seq_total)
    return (
        jnp.exp(-(decay_rate[:, None] * positions[None, :]) / seq_total) / jnp.sqrt(energy)[:, None]
    )


def featurize_rim(signal, before, kernel):
    extended = jnp.concatenate([before, signal], axis=1).astype(jnp.float32)
    num_taps = kernel.shape[1]
    rim_len = num_taps - 1
    num_tok = signal.shape[1]
    result = kernel[:, 0:1] * extended[:, rim_len:]
    for offset in range(1, num_taps):
        result = (
            result
            + kernel[:, offset : offset + 1]
            * extended[:, rim_len - offset : rim_len - offset + num_tok]
        )
    return result


def featurize_back(signal, following, kernel):
    extended = jnp.concatenate([signal, following], axis=1).astype(jnp.float32)
    num_taps = kernel.shape[1]
    num_tok = signal.shape[1]
    result = kernel[:, 0:1] * extended[:, :num_tok]
    for offset in range(1, num_taps):
        result = result + kernel[:, offset : offset + 1] * extended[:, offset : offset + num_tok]
    return result


def tables(num_rows, num_cols, modulus):
    row_ids = jnp.arange(num_rows, dtype=jnp.int32)[:, None]
    col_ids = jnp.arange(num_cols, dtype=jnp.int32)[None, :]
    angles = (row_ids * col_ids % modulus).astype(jnp.float32) * (-2.0 * math.pi / modulus)
    return (jnp.cos(angles), jnp.sin(angles))


def spectrum(signal, outer, twiddle, inner):
    num_chan = signal.shape[0]
    folded = signal.reshape(num_chan, outer[0].shape[1], inner[0].shape[0])
    section_re = jnp.einsum("kt,nts->nks", outer[0], folded, precision=PRECISE)
    section_im = jnp.einsum("kt,nts->nks", outer[1], folded, precision=PRECISE)
    turned_re = section_re * twiddle[0] - section_im * twiddle[1]
    turned_im = section_re * twiddle[1] + section_im * twiddle[0]
    spec_re = jnp.einsum("nks,sj->nkj", turned_re, inner[0], precision=PRECISE) - jnp.einsum(
        "nks,sj->nkj", turned_im, inner[1], precision=PRECISE
    )
    spec_im = jnp.einsum("nks,sj->nkj", turned_re, inner[1], precision=PRECISE) + jnp.einsum(
        "nks,sj->nkj", turned_im, inner[0], precision=PRECISE
    )
    return (spec_re, spec_im)


def restore(spec_re, spec_im, outer, twiddle, inner):
    num_chan = spec_re.shape[0]
    padded_len = outer[0].shape[0] * inner[0].shape[0]
    back_re = jnp.einsum("nkj,sj->nks", spec_re, inner[0], precision=PRECISE) + jnp.einsum(
        "nkj,sj->nks", spec_im, inner[1], precision=PRECISE
    )
    back_im = jnp.einsum("nkj,sj->nks", spec_im, inner[0], precision=PRECISE) - jnp.einsum(
        "nkj,sj->nks", spec_re, inner[1], precision=PRECISE
    )
    turned_re = back_re * twiddle[0] + back_im * twiddle[1]
    turned_im = back_im * twiddle[0] - back_re * twiddle[1]
    result = jnp.einsum("kt,nks->nts", outer[0], turned_re, precision=PRECISE) + jnp.einsum(
        "kt,nks->nts", outer[1], turned_im, precision=PRECISE
    )
    return result.reshape(num_chan, -1) * (1.0 / padded_len)


def convolve_forward(carried_chan, filter_chan, own_skip, transform_tables):
    outer, twiddle, inner = transform_tables
    carried_wide = carried_chan.astype(jnp.float32)
    carried_re, carried_im = spectrum(carried_wide, outer, twiddle, inner)
    filter_re, filter_im = spectrum(filter_chan.astype(jnp.float32), outer, twiddle, inner)
    conv_chan = restore(
        filter_re * carried_re - filter_im * carried_im,
        filter_re * carried_im + filter_im * carried_re,
        outer,
        twiddle,
        inner,
    )
    long_chan = (conv_chan + own_skip[:, None] * carried_wide).astype(jnp.bfloat16)
    return (long_chan, (carried_re, carried_im, filter_re, filter_im))


def convolve_backward(grad_chan, spectra, own_skip, transform_tables):
    outer, twiddle, inner = transform_tables
    carried_re, carried_im, filter_re, filter_im = spectra
    grad_chan_wide = grad_chan.astype(jnp.float32)
    grad_re, grad_im = spectrum(grad_chan_wide, outer, twiddle, inner)
    carried_grad_chan = (
        restore(
            filter_re * grad_re + filter_im * grad_im,
            filter_re * grad_im - filter_im * grad_re,
            outer,
            twiddle,
            inner,
        )
        + own_skip[:, None] * grad_chan_wide
    ).astype(jnp.bfloat16)
    filter_grad_chan = restore(
        carried_re * grad_re + carried_im * grad_im,
        carried_re * grad_im - carried_im * grad_re,
        outer,
        twiddle,
        inner,
    ).astype(jnp.bfloat16)
    return (carried_grad_chan, filter_grad_chan)


def on_device(
    query_in,
    key_in,
    value_in,
    short_kernel,
    basis_weight,
    basis_bias,
    filter_proj,
    decay_rate,
    skip_gain,
    grad_out,
):
    ctx_size = lax.axis_size("ctx")
    ctx_rank = lax.axis_index("ctx")
    tp_size = lax.axis_size("tp")
    num_tok = query_in.shape[1]
    chan_local = query_in.shape[0]
    seq_total = num_tok * ctx_size
    all_channels = chan_local * tp_size
    num_freq = (basis_weight.shape[1] - 1) // 2
    feat_width = basis_weight.shape[0]
    rim_len = short_kernel.shape[2] - 1
    tok_start = ctx_rank * num_tok
    rim_edge = num_tok - rim_len
    per_dev = chan_local // ctx_size
    chan_start = ctx_rank * per_dev
    own_skip = lax.dynamic_slice_in_dim(skip_gain, chan_start, per_dev)
    proj_scale = 1.0 / math.sqrt(seq_total)
    basis_scale = math.sqrt(feat_width / (seq_total * all_channels))
    before = passed_along(
        (query_in[:, rim_edge:], key_in[:, rim_edge:], value_in[:, rim_edge:]), "ctx", 1
    )
    query_feat = featurize_rim(query_in, before[0], short_kernel[0])
    key_feat = featurize_rim(key_in, before[1], short_kernel[1])
    value_feat = featurize_rim(value_in, before[2], short_kernel[2])
    carried = (key_feat * value_feat).astype(jnp.bfloat16)
    grad_wide = grad_out.astype(jnp.float32)
    grad_long = (grad_wide * query_feat).astype(jnp.bfloat16)
    basis_rows = features(tok_start, num_tok, seq_total, num_freq)
    hidden_in = (
        jnp.dot(basis_weight, basis_rows, precision=PRECISE, preferred_element_type=jnp.float32)
        + basis_bias[:, None]
    )
    activation = jnp.sin(hidden_in)
    envelope = window(decay_rate, tok_start, num_tok, seq_total)
    filter_tok = (
        jnp.dot(filter_proj, activation, precision=PRECISE, preferred_element_type=jnp.float32)
        * envelope
    ).astype(jnp.bfloat16)
    inner_len = 2 * ctx_size
    transform_tables = (
        tables(num_tok, num_tok // 2, num_tok),
        tables(num_tok, inner_len, 2 * seq_total),
        tables(inner_len, inner_len, inner_len),
    )
    spread = (
        lax.all_to_all(carried, "ctx", split_axis=0, concat_axis=1, tiled=True),
        lax.all_to_all(filter_tok, "ctx", split_axis=0, concat_axis=1, tiled=True),
    )
    carried_chan = spread[0]
    filter_chan = spread[1]
    long_chan, spectra = convolve_forward(carried_chan, filter_chan, own_skip, transform_tables)
    long_tok = lax.all_to_all(long_chan, "ctx", split_axis=1, concat_axis=0, tiled=True)
    grad_chan = lax.all_to_all(grad_long, "ctx", split_axis=0, concat_axis=1, tiled=True)
    carried_grad_chan, filter_grad_chan = convolve_backward(
        grad_chan, spectra, own_skip, transform_tables
    )
    returned = (
        lax.all_to_all(carried_grad_chan, "ctx", split_axis=1, concat_axis=0, tiled=True),
        lax.all_to_all(filter_grad_chan, "ctx", split_axis=1, concat_axis=0, tiled=True),
    )
    carried_grad = returned[0]
    filter_grad_tok = returned[1]
    long_wide = long_tok.astype(jnp.float32)
    mixed = (query_feat * long_wide).astype(jnp.bfloat16)
    grad_query_feat = (grad_wide * long_wide).astype(jnp.bfloat16)
    grad_raw = filter_grad_tok.astype(jnp.float32) * envelope
    part_proj = jnp.dot(
        grad_raw, activation.T, precision=PRECISE, preferred_element_type=jnp.float32
    )
    grad_hidden = jnp.dot(
        filter_proj.T, grad_raw, precision=PRECISE, preferred_element_type=jnp.float32
    ) * jnp.cos(hidden_in)
    part_basis = jnp.dot(
        grad_hidden, basis_rows.T, precision=PRECISE, preferred_element_type=jnp.float32
    )
    grad_proj = lax.psum(part_proj, "ctx") * proj_scale
    grad_basis = lax.psum(part_basis, ("ctx", "tp")) * basis_scale
    carried_grad_wide = carried_grad.astype(jnp.float32)
    grad_key_feat = (carried_grad_wide * value_feat).astype(jnp.bfloat16)
    grad_value_feat = (carried_grad_wide * key_feat).astype(jnp.bfloat16)
    following = passed_along(
        (grad_query_feat[:, :rim_len], grad_key_feat[:, :rim_len], grad_value_feat[:, :rim_len]),
        "ctx",
        -1,
    )
    grad_query = featurize_back(grad_query_feat, following[0], short_kernel[0]).astype(jnp.bfloat16)
    grad_key = featurize_back(grad_key_feat, following[1], short_kernel[1]).astype(jnp.bfloat16)
    grad_value = featurize_back(grad_value_feat, following[2], short_kernel[2]).astype(jnp.bfloat16)
    return (mixed, grad_query, grad_key, grad_value, grad_proj, grad_basis)


def solution(mesh):
    return jax.shard_map(
        on_device,
        mesh=mesh,
        in_specs=(
            P("tp", "ctx"),
            P("tp", "ctx"),
            P("tp", "ctx"),
            P(None, "tp", None),
            P(),
            P(),
            P("tp", None),
            P("tp"),
            P("tp"),
            P("tp", "ctx"),
        ),
        out_specs=(
            P("tp", "ctx"),
            P("tp", "ctx"),
            P("tp", "ctx"),
            P("tp", "ctx"),
            P("tp", None),
            P(),
        ),
        check_vma=False,
    )
```

profile of v0, /device:TPU:1, one launch (start us, length us, event | category | flops | bytes accessed | tf_op | source)
XLA Modules:
  0.0 538.5 jit_solution(8369667688324918726)
XLA Ops:
  0.6 0.8 slice.242
  1.5 4.6 collective-permute-start
  10.4 15.5 %all-to-all-start = ((bf16[64,2,256]{2,1,0:T(2,128)(2,1)}), bf16[64,2,256]{2,1,0:T(2,128)(2,1)S(1)}, u32[]{:S(2)}, u32[]{:S(2)}) async-start(bf16[64,2,256]{2,1,0:T(2,128)(2,1)} %all_to_all.60), calls=%async_computation | async-start | bytes 131072 | tf_op jit(solution)/shard_map/all_to_all | solution.py:199
  26.0 3.5 collective-permute-start.2
  29.6 2.2 collective-permute-start.1
  35.7 2.4 all-to-all-done
  38.1 9.7 %all-to-all-start.3 = ((bf16[64,2,256]{2,1,0:T(2,128)(2,1)}), bf16[64,2,256]{2,1,0:T(2,128)(2,1)S(1)}, u32[]{:S(2)}, u32[]{:S(2)}) async-start(bf16[64,2,256]{2,1,0:T(2,128)(2,1)} %all_to_all.67), calls=%async_computation.3 | async-start | bytes 131072 | tf_op jit(solution)/shard_map/all_to_all | solution.py:205
  47.8 0.8 convolution_bitcast_fusion.4
  48.6 0.8 convolution_bitcast_fusion.5
  49.4 0.8 fusion.144
  50.1 0.8 convolution_subtract_fusion.5
  50.9 0.8 fusion.121
  51.7 7.9 %all-to-all-done.3 = bf16[64,2,256]{2,1,0:T(2,128)(2,1)S(1)} async-done(((bf16[64,2,256]{2,1,0:T(2,128)(2,1)}), bf16[64,2,256]{2,1,0:T(2,128)(2,1)S(1)}, u32[]{:S(2)}, u32[]{:S(2)}) %all-to-all-start.3) | async-done | bytes 65568 | tf_op jit(solution)/shard_map/all_to_all | solution.py:205
  59.6 0.8 convolution_bitcast_fusion
  60.4 0.8 convolution_bitcast_fusion.1
  61.2 0.8 fusion.134
  62.0 0.8 fusion.114
  62.7 0.8 convolution_subtract_fusion.2
  63.5 0.8 convolution_add_fusion.2
  64.3 0.8 multiply_add_fusion.1
  67.6 11.5 %fusion.19 = f32[2,128,128]{2,1,0:T(8,128)S(1)} fusion(f32[2,256,128]{1,2,0:T(8,128)S(1)} %convolution_subtract_fusion.1, f32[2,256,128]{1,2,0:T(8,128)S(1)} %convolution_add_fusion.1, f32[256,128]{0,1:T(8,128)S(1)} %copy.206, f32[256,128]{0,1:T(8,128)S(1)} %copy.204), kind=kOutput, calls=%fused_computation.45 | convolution fusion | flops 101318656 | bytes 917504 | tf_op jit(solution)/shard_map/kt,nks->nts/dot_general | solution.py:95
  79.1 0.9 fusion.2
  80.9 4.8 all-to-all-start.4
  86.0 12.0 %all-to-all-done.4 = bf16[2,64,256]{2,0,1:T(2,128)(2,1)S(1)} async-done(((bf16[2,64,256]{2,0,1:T(2,128)(2,1)}), bf16[2,64,256]{2,0,1:T(2,128)(2,1)S(1)}, u32[]{:S(2)}, u32[]{:S(2)}) %all-to-all-start.4) | async-done | bytes 65568 | tf_op jit(solution)/shard_map/all_to_all | solution.py:210
  98.5 2.3 collective-permute-start.5
  101.9 6.0 %all-to-all-start.1 = ((bf16[64,2,256]{2,1,0:T(2,128)(2,1)}), bf16[64,2,256]{2,1,0:T(2,128)(2,1)S(1)}, u32[]{:S(2)}, u32[]{:S(2)}) async-start(bf16[64,2,256]{2,1,0:T(2,128)(2,1)} %all_to_all.63), calls=%async_computation.1 | async-start | bytes 131072 | tf_op jit(solution)/shard_map/all_to_all | solution.py:198
  108.0 2.4 collective-permute-start.4
  110.4 1.0 fusion.37
  111.4 2.1 collective-permute-done.4
  113.5 1.0 fusion.44
  114.5 5.6 %all-to-all-done.1 = bf16[64,2,256]{2,1,0:T(2,128)(2,1)S(1)} async-done(((bf16[64,2,256]{2,1,0:T(2,128)(2,1)}), bf16[64,2,256]{2,1,0:T(2,128)(2,1)S(1)}, u32[]{:S(2)}, u32[]{:S(2)}) %all-to-all-start.1) | async-done | bytes 65568 | tf_op jit(solution)/shard_map/all_to_all | solution.py:198
  120.2 0.8 convolution_bitcast_fusion.2
  121.0 0.8 convolution_bitcast_fusion.3
  121.8 0.8 fusion.119
  122.5 0.8 fusion.142
  123.3 0.8 convolution_subtract_fusion.4
  124.0 0.8 multiply_add_fusion
  127.4 0.9 fusion.12
  128.3 0.9 fusion.8
  130.0 7.0 %all-to-all-start.5 = ((bf16[2,64,256]{2,0,1:T(2,128)(2,1)}), bf16[2,64,256]{2,0,1:T(2,128)(2,1)S(1)}, u32[]{:S(2)}, u32[]{:S(2)}) async-start(bf16[2,64,256]{2,0,1:T(2,128)(2,1)} %copy.242), calls=%async_computation.5 | async-start | bytes 131072 | tf_op jit(solution)/shard_map/all_to_all | solution.py:211
  139.6 0.9 fusion.26
  140.5 0.9 fusion.4
  142.3 6.9 %all-to-all-done.5 = bf16[2,64,256]{2,0,1:T(2,128)(2,1)S(1)} async-done(((bf16[2,64,256]{2,0,1:T(2,128)(2,1)}), bf16[2,64,256]{2,0,1:T(2,128)(2,1)S(1)}, u32[]{:S(2)}, u32[]{:S(2)}) %all-to-all-start.5) | async-done | bytes 65568 | tf_op jit(solution)/shard_map/all_to_all | solution.py:211
  149.2 5.8 %all-to-all-start.2 = ((bf16[2,64,256]{2,0,1:T(2,128)(2,1)}), bf16[2,64,256]{2,0,1:T(2,128)(2,1)S(1)}, u32[]{:S(2)}, u32[]{:S(2)}) async-start(bf16[2,64,256]{2,0,1:T(2,128)(2,1)} %copy.223), calls=%async_computation.2 | async-start | bytes 131072 | tf_op jit(solution)/shard_map/all_to_all | solution.py:204
  156.2 99.6 %psum.15 = f32[64,33]{0,1:T(8,128)S(1)} all-reduce(f32[64,33]{0,1:T(8,128)S(1)} %fusion.423), channel_id=1, replica_groups=mesh['ctx'=64,'tp'=8] {'ctx','tp'}, use_global_device_ids=true, to_apply=%region_1.2 | all-reduce | flops 2112 | bytes 16896 | tf_op jit(solution)/shard_map/psum | solution.py:229
  255.8 270.7 %psum.14 = f32[128,64]{0,1:T(8,128)S(1)} all-reduce(f32[128,64]{0,1:T(8,128)S(1)} %fusion.417), channel_id=1, replica_groups=mesh['ctx'=64,'tp'=8] {'ctx'}, use_global_device_ids=true, to_apply=%region_0.1 | all-reduce | flops 8192 | bytes 65536 | tf_op jit(solution)/shard_map/psum | solution.py:228
  528.0 8.4 %collective-permute-start.3 = (bf16[128,6]{1,0:T(8,128)(2,1)S(1)}, bf16[128,6]{1,0:T(8,128)(2,1)S(1)}, u32[]{:S(2)}, u32[]{:S(2)}) collective-permute-start(bf16[128,6]{1,0:T(8,128)(2,1)S(1)} %slice.333), channel_id=1, source_target_pairs={{8,0},{16,8},{24,16},{32,24},{40,32},{48,40},{56,48},{64,56},{72,6... | collective-permute-start | bytes 4616 | tf_op jit(solution)/shard_map/ppermute | solution.py:13
  537.3 1.0 fusion.51
  (116 shorter events, 23.9 us)
Async XLA Ops:
  0.6 8.8 %copy-start = (f32[128,64]{0,1:T(8,128)S(1)}, f32[128,64]{0,1:T(8,128)}, u32[]{:S(2)}) copy-start(f32[128,64]{0,1:T(8,128)} %param.16) | copy-start | bytes 98308
  1.5 32.3 %collective-permute-start = (bf16[128,6]{1,0:T(8,128)(2,1)S(1)}, bf16[128,6]{1,0:T(8,128)(2,1)S(1)}, u32[]{:S(2)}, u32[]{:S(2)}) collective-permute-start(bf16[128,6]{1,0:T(8,128)(2,1)S(1)} %slice.242), channel_id=1, source_target_pairs={{0,8},{8,16},{16,24},{24,32},{32,40},{40,48},{48,56},{56,64},{64,7... | collective-permute-start | bytes 4616 | tf_op jit(solution)/shard_map/ppermute | solution.py:13
  7.5 0.7 copy-start.9
  8.2 0.7 copy-start.5
  8.2 0.7 copy-start.7
  10.4 15.5 %copy-start.3 = (bf16[128,256]{1,0:T(8,128)(2,1)S(1)}, bf16[128,256]{1,0:T(8,128)(2,1)}, u32[]{:S(2)}) copy-start(bf16[128,256]{1,0:T(8,128)(2,1)} %param.12) | copy-start | bytes 196612
  10.4 27.7 %all-to-all-start = ((bf16[64,2,256]{2,1,0:T(2,128)(2,1)}), bf16[64,2,256]{2,1,0:T(2,128)(2,1)S(1)}, u32[]{:S(2)}, u32[]{:S(2)}) async-start(bf16[64,2,256]{2,1,0:T(2,128)(2,1)} %all_to_all.60), calls=%async_computation | async-start | bytes 131072 | tf_op jit(solution)/shard_map/all_to_all | solution.py:199
  25.9 3.6 copy-start.4
  26.0 59.8 %collective-permute-start.2 = (bf16[128,6]{1,0:T(8,128)(2,1)S(1)}, bf16[128,6]{1,0:T(8,128)(2,1)S(1)}, u32[]{:S(2)}, u32[]{:S(2)}) collective-permute-start(bf16[128,6]{1,0:T(8,128)(2,1)S(1)} %slice.274), channel_id=1, source_target_pairs={{0,8},{8,16},{16,24},{24,32},{32,40},{40,48},{48,56},{56,64},{64,7... | collective-permute-start | bytes 4616 | tf_op jit(solution)/shard_map/ppermute | solution.py:13
  29.6 2.7 copy-start.6
  29.6 56.3 %collective-permute-start.1 = (bf16[128,6]{1,0:T(8,128)(2,1)S(1)}, bf16[128,6]{1,0:T(8,128)(2,1)S(1)}, u32[]{:S(2)}, u32[]{:S(2)}) collective-permute-start(bf16[128,6]{1,0:T(8,128)(2,1)S(1)} %slice.258), channel_id=1, source_target_pairs={{0,8},{8,16},{16,24},{24,32},{32,40},{40,48},{48,56},{56,64},{64,7... | collective-permute-start | bytes 4616 | tf_op jit(solution)/shard_map/ppermute | solution.py:13
  33.0 0.9 copy-start.2
  33.1 0.7 copy-start.8
  33.8 0.8 copy-start.1
  38.1 21.5 %all-to-all-start.3 = ((bf16[64,2,256]{2,1,0:T(2,128)(2,1)}), bf16[64,2,256]{2,1,0:T(2,128)(2,1)S(1)}, u32[]{:S(2)}, u32[]{:S(2)}) async-start(bf16[64,2,256]{2,1,0:T(2,128)(2,1)} %all_to_all.67), calls=%async_computation.3 | async-start | bytes 131072 | tf_op jit(solution)/shard_map/all_to_all | solution.py:205
  80.9 17.0 %all-to-all-start.4 = ((bf16[2,64,256]{2,0,1:T(2,128)(2,1)}), bf16[2,64,256]{2,0,1:T(2,128)(2,1)S(1)}, u32[]{:S(2)}, u32[]{:S(2)}) async-start(bf16[2,64,256]{2,0,1:T(2,128)(2,1)} %copy.236), calls=%async_computation.4 | async-start | bytes 131072 | tf_op jit(solution)/shard_map/all_to_all | solution.py:210
  98.5 11.8 %collective-permute-start.5 = (bf16[128,6]{1,0:T(8,128)(2,1)S(1)}, bf16[128,6]{1,0:T(8,128)(2,1)S(1)}, u32[]{:S(2)}, u32[]{:S(2)}) collective-permute-start(bf16[128,6]{1,0:T(8,128)(2,1)S(1)} %slice.349), channel_id=1, source_target_pairs={{8,0},{16,8},{24,16},{32,24},{40,32},{48,40},{56,48},{64,56},{72,6... | collective-permute-start | bytes 4616 | tf_op jit(solution)/shard_map/ppermute | solution.py:13
  101.9 18.2 %all-to-all-start.1 = ((bf16[64,2,256]{2,1,0:T(2,128)(2,1)}), bf16[64,2,256]{2,1,0:T(2,128)(2,1)S(1)}, u32[]{:S(2)}, u32[]{:S(2)}) async-start(bf16[64,2,256]{2,1,0:T(2,128)(2,1)} %all_to_all.63), calls=%async_computation.1 | async-start | bytes 131072 | tf_op jit(solution)/shard_map/all_to_all | solution.py:198
  108.0 5.5 %collective-permute-start.4 = (bf16[128,6]{1,0:T(8,128)(2,1)S(1)}, bf16[128,6]{1,0:T(8,128)(2,1)S(1)}, u32[]{:S(2)}, u32[]{:S(2)}) collective-permute-start(bf16[128,6]{1,0:T(8,128)(2,1)S(1)} %slice.341), channel_id=1, source_target_pairs={{8,0},{16,8},{24,16},{32,24},{40,32},{48,40},{56,48},{64,56},{72,6... | collective-permute-start | bytes 4616 | tf_op jit(solution)/shard_map/ppermute | solution.py:13
  130.0 19.1 %all-to-all-start.5 = ((bf16[2,64,256]{2,0,1:T(2,128)(2,1)}), bf16[2,64,256]{2,0,1:T(2,128)(2,1)S(1)}, u32[]{:S(2)}, u32[]{:S(2)}) async-start(bf16[2,64,256]{2,0,1:T(2,128)(2,1)} %copy.242), calls=%async_computation.5 | async-start | bytes 131072 | tf_op jit(solution)/shard_map/all_to_all | solution.py:211
  149.2 378.0 %all-to-all-start.2 = ((bf16[2,64,256]{2,0,1:T(2,128)(2,1)}), bf16[2,64,256]{2,0,1:T(2,128)(2,1)S(1)}, u32[]{:S(2)}, u32[]{:S(2)}) async-start(bf16[2,64,256]{2,0,1:T(2,128)(2,1)} %copy.223), calls=%async_computation.2 | async-start | bytes 131072 | tf_op jit(solution)/shard_map/all_to_all | solution.py:204
  528.0 9.3 %collective-permute-start.3 = (bf16[128,6]{1,0:T(8,128)(2,1)S(1)}, bf16[128,6]{1,0:T(8,128)(2,1)S(1)}, u32[]{:S(2)}, u32[]{:S(2)}) collective-permute-start(bf16[128,6]{1,0:T(8,128)(2,1)S(1)} %slice.333), channel_id=1, source_target_pairs={{8,0},{16,8},{24,16},{32,24},{40,32},{48,40},{56,48},{64,56},{72,6... | collective-permute-start | bytes 4616 | tf_op jit(solution)/shard_map/ppermute | solution.py:13
where the time goes:
time: 544 us; the launch traced here: 539 us
  blocking collectives  370 us (68%)
  starting transfers between devices  72.2 us (13%)
  matrix products  39.1 us (7%)
  waiting for transfers between devices  37.1 us (7%)
  other arithmetic  9.16 us (2%)
  local copies, waits for them, and re-layouts  8.96 us (2%)
    psum x1, blocking collectives, on_device(): grad_proj = lax.psum(part_proj, 'ctx') * proj_scale  271 us
    psum x1, blocking collectives, on_device(): grad_basis = lax.psum(part_basis, ('ctx', 'tp')) * basis_scale  99.6 us
    ppermute x6, starting transfers between devices, passed_along(): lax.ppermute(value, axis, [(source, source + steps) for source in range(l...  23.4 us
    all_to_all x1, starting transfers between devices, on_device(): lax.all_to_all(filter_tok, 'ctx', split_axis=0, concat_axis=1, tiled=True)  15.5 us
    dot_general x3, matrix products, restore(): jnp.einsum('kt,nks->nts', outer[0], turned_re, precision=PRECISE)  13.3 us
    all_to_all x1, waiting for transfers between devices, on_device(): lax.all_to_all(carried_grad_chan, 'ctx', split_axis=1, concat_axis=0, til...  12 us
  transfers between devices with their start and end apart: 12, of which 7 were waited for; matrix products, arithmetic and copies ran while one was open for 7% of the time, Pallas kernels for 0%

commit v1 on v0

--- a/solution.py
+++ b/solution.py
@@ -208,7 +208,12 @@
     )
     returned = (
         lax.all_to_all(carried_grad_chan, "ctx", split_axis=1, concat_axis=0, tiled=True),
-        lax.all_to_all(filter_grad_chan, "ctx", split_axis=1, concat_axis=0, tiled=True),
+        jnp.concatenate(
+            lax.all_to_all(
+                jnp.stack(jnp.split(filter_grad_chan, lax.axis_size("ctx"), axis=1)), "ctx", 0, 0
+            ),
+            axis=0,
+        ),
     )
     carried_grad = returned[0]
     filter_grad_tok = returned[1]

time: 544 us -> 580 us (1.066)
  local copies, waits for them, and re-layouts: 8.96 us -> 44.4 us
    unnamed x20 -> x84, local copies, waits for them, and re-layouts: 2.66 us -> 38.3 us
where the time goes in v1:
time: 580 us; the launch traced here: 574 us
  blocking collectives  370 us (64%)
  starting transfers between devices  72.2 us (12%)
  local copies, waits for them, and re-layouts  44.4 us (8%)
  matrix products  39.4 us (7%)
  waiting for transfers between devices  37.1 us (6%)
  other arithmetic  9.12 us (2%)
    psum x1, blocking collectives, on_device(): grad_proj = lax.psum(part_proj, 'ctx') * proj_scale  271 us
    psum x1, blocking collectives, on_device(): grad_basis = lax.psum(part_basis, ('ctx', 'tp')) * basis_scale  99.6 us
    unnamed x84, local copies, waits for them, and re-layouts  38.3 us
    ppermute x6, starting transfers between devices, passed_along(): lax.ppermute(value, axis, [(source, source + steps) for source in range(l...  23.4 us
    all_to_all x1, starting transfers between devices, on_device(): lax.all_to_all(filter_tok, 'ctx', split_axis=0, concat_axis=1, tiled=True)  15.5 us
    dot_general x3, matrix products, restore(): jnp.einsum('kt,nks->nts', outer[0], turned_re, precision=PRECISE)  13.6 us
    all_to_all x1, waiting for transfers between devices, on_device(): lax.all_to_all(carried_grad_chan, 'ctx', split_axis=1, concat_axis=0, til...  12 us
  transfers between devices with their start and end apart: 12, of which 7 were waited for; matrix products, arithmetic and copies ran while one was open for 7% of the time, Pallas kernels for 0%

profile of v1, /device:TPU:1, one launch (start us, length us, event | category | flops | bytes accessed | tf_op | source)
XLA Modules:
  0.0 574.3 jit_solution(5328795821849559709)
XLA Ops:
  0.6 0.8 slice.242
  1.5 4.6 collective-permute-start
  10.4 15.5 %all-to-all-start = ((bf16[64,2,256]{2,1,0:T(2,128)(2,1)}), bf16[64,2,256]{2,1,0:T(2,128)(2,1)S(1)}, u32[]{:S(2)}, u32[]{:S(2)}) async-start(bf16[64,2,256]{2,1,0:T(2,128)(2,1)} %all_to_all.55), calls=%async_computation | async-start | bytes 131072 | tf_op jit(solution)/shard_map/all_to_all | solution.py:199
  26.0 3.5 collective-permute-start.2
  29.6 2.2 collective-permute-start.1
  35.7 2.4 all-to-all-done
  38.1 9.7 %all-to-all-start.3 = ((bf16[64,2,256]{2,1,0:T(2,128)(2,1)}), bf16[64,2,256]{2,1,0:T(2,128)(2,1)S(1)}, u32[]{:S(2)}, u32[]{:S(2)}) async-start(bf16[64,2,256]{2,1,0:T(2,128)(2,1)} %all_to_all.62), calls=%async_computation.3 | async-start | bytes 131072 | tf_op jit(solution)/shard_map/all_to_all | solution.py:205
  47.8 0.8 convolution_bitcast_fusion.4
  48.6 0.8 convolution_bitcast_fusion.5
  49.4 0.8 fusion.144
  50.1 0.8 convolution_subtract_fusion.5
  50.9 0.8 fusion.121
  51.7 7.9 %all-to-all-done.3 = bf16[64,2,256]{2,1,0:T(2,128)(2,1)S(1)} async-done(((bf16[64,2,256]{2,1,0:T(2,128)(2,1)}), bf16[64,2,256]{2,1,0:T(2,128)(2,1)S(1)}, u32[]{:S(2)}, u32[]{:S(2)}) %all-to-all-start.3) | async-done | bytes 65568 | tf_op jit(solution)/shard_map/all_to_all | solution.py:205
  59.6 0.8 convolution_bitcast_fusion
  60.4 0.8 convolution_bitcast_fusion.1
  61.2 0.8 fusion.134
  62.0 0.8 fusion.114
  62.7 0.8 convolution_subtract_fusion.2
  63.5 0.8 convolution_add_fusion.2
  64.3 0.8 multiply_add_fusion.1
  67.6 11.9 %fusion.19 = f32[2,128,128]{2,1,0:T(8,128)S(1)} fusion(f32[2,256,128]{1,2,0:T(8,128)S(1)} %convolution_subtract_fusion.1, f32[2,256,128]{1,2,0:T(8,128)S(1)} %convolution_add_fusion.1, f32[256,128]{0,1:T(8,128)S(1)} %copy.202, f32[256,128]{0,1:T(8,128)S(1)} %copy.200), kind=kOutput, calls=%fused_computation.45 | convolution fusion | flops 101318656 | bytes 917504 | tf_op jit(solution)/shard_map/kt,nks->nts/dot_general | solution.py:95
  79.5 0.9 fusion.2
  81.3 4.8 all-to-all-start.4
  86.4 12.0 %all-to-all-done.4 = bf16[2,64,256]{2,0,1:T(2,128)(2,1)S(1)} async-done(((bf16[2,64,256]{2,0,1:T(2,128)(2,1)}), bf16[2,64,256]{2,0,1:T(2,128)(2,1)S(1)}, u32[]{:S(2)}, u32[]{:S(2)}) %all-to-all-start.4) | async-done | bytes 65568 | tf_op jit(solution)/shard_map/all_to_all | solution.py:210
  98.9 2.3 collective-permute-start.5
  102.3 6.0 %all-to-all-start.1 = ((bf16[64,2,256]{2,1,0:T(2,128)(2,1)}), bf16[64,2,256]{2,1,0:T(2,128)(2,1)S(1)}, u32[]{:S(2)}, u32[]{:S(2)}) async-start(bf16[64,2,256]{2,1,0:T(2,128)(2,1)} %all_to_all.58), calls=%async_computation.1 | async-start | bytes 131072 | tf_op jit(solution)/shard_map/all_to_all | solution.py:198
  108.3 2.4 collective-permute-start.4
  110.7 1.0 fusion.37
  111.8 2.1 collective-permute-done.4
  113.9 1.0 fusion.44
  114.9 5.6 all-to-all-done.1
  120.5 0.8 convolution_bitcast_fusion.2
  121.3 0.8 convolution_bitcast_fusion.3
  122.1 0.8 fusion.119
  122.9 0.8 fusion.142
  123.6 0.8 convolution_subtract_fusion.4
  124.4 0.8 multiply_add_fusion
  127.8 0.9 fusion.12
  128.7 0.9 fusion.8
  165.9 7.0 %all-to-all-start.5 = ((bf16[64,2,256]{2,1,0:T(2,128)(2,1)}), bf16[64,2,256]{2,1,0:T(2,128)(2,1)S(1)}, u32[]{:S(2)}, u32[]{:S(2)}) async-start(bf16[64,2,256]{2,1,0:T(2,128)(2,1)} %constant_dynamic-update-slice_fusion), calls=%async_computation.5 | async-start | bytes 131072 | tf_op jit(solution)/shard_map/all_to_all | solution.py:212
  175.5 0.9 fusion.26
  176.3 0.9 fusion.4
  178.1 6.9 %all-to-all-done.5 = bf16[64,2,256]{2,1,0:T(2,128)(2,1)S(1)} async-done(((bf16[64,2,256]{2,1,0:T(2,128)(2,1)}), bf16[64,2,256]{2,1,0:T(2,128)(2,1)S(1)}, u32[]{:S(2)}, u32[]{:S(2)}) %all-to-all-start.5) | async-done | bytes 65568 | tf_op jit(solution)/shard_map/all_to_all | solution.py:212
  185.1 5.8 %all-to-all-start.2 = ((bf16[2,64,256]{2,0,1:T(2,128)(2,1)}), bf16[2,64,256]{2,0,1:T(2,128)(2,1)S(1)}, u32[]{:S(2)}, u32[]{:S(2)}) async-start(bf16[2,64,256]{2,0,1:T(2,128)(2,1)} %copy.219), calls=%async_computation.2 | async-start | bytes 131072 | tf_op jit(solution)/shard_map/all_to_all | solution.py:204
  191.9 99.6 %psum.15 = f32[64,33]{0,1:T(8,128)S(1)} all-reduce(f32[64,33]{0,1:T(8,128)S(1)} %fusion.423), channel_id=1, replica_groups=mesh['ctx'=64,'tp'=8] {'ctx','tp'}, use_global_device_ids=true, to_apply=%region_1.2 | all-reduce | flops 2112 | bytes 16896 | tf_op jit(solution)/shard_map/psum | solution.py:234
  291.6 270.7 %psum.14 = f32[128,64]{0,1:T(8,128)S(1)} all-reduce(f32[128,64]{0,1:T(8,128)S(1)} %fusion.417), channel_id=1, replica_groups=mesh['ctx'=64,'tp'=8] {'ctx'}, use_global_device_ids=true, to_apply=%region_0.1 | all-reduce | flops 8192 | bytes 65536 | tf_op jit(solution)/shard_map/psum | solution.py:233
  563.7 8.4 %collective-permute-start.3 = (bf16[128,6]{1,0:T(8,128)(2,1)S(1)}, bf16[128,6]{1,0:T(8,128)(2,1)S(1)}, u32[]{:S(2)}, u32[]{:S(2)}) collective-permute-start(bf16[128,6]{1,0:T(8,128)(2,1)S(1)} %slice.333), channel_id=1, source_target_pairs={{8,0},{16,8},{24,16},{32,24},{40,32},{48,40},{56,48},{64,56},{72,6... | collective-permute-start | bytes 4616 | tf_op jit(solution)/shard_map/ppermute | solution.py:13
  573.0 1.0 fusion.51
  (178 shorter events, 59.2 us)
Async XLA Ops:
  0.6 8.8 %copy-start = (f32[128,64]{0,1:T(8,128)S(1)}, f32[128,64]{0,1:T(8,128)}, u32[]{:S(2)}) copy-start(f32[128,64]{0,1:T(8,128)} %param.16) | copy-start | bytes 98308
  1.5 32.3 %collective-permute-start = (bf16[128,6]{1,0:T(8,128)(2,1)S(1)}, bf16[128,6]{1,0:T(8,128)(2,1)S(1)}, u32[]{:S(2)}, u32[]{:S(2)}) collective-permute-start(bf16[128,6]{1,0:T(8,128)(2,1)S(1)} %slice.242), channel_id=1, source_target_pairs={{0,8},{8,16},{16,24},{24,32},{32,40},{40,48},{48,56},{56,64},{64,7... | collective-permute-start | bytes 4616 | tf_op jit(solution)/shard_map/ppermute | solution.py:13
  7.5 0.7 copy-start.9
  8.2 0.7 copy-start.5
  8.2 0.7 copy-start.7
  10.4 15.5 %copy-start.3 = (bf16[128,256]{1,0:T(8,128)(2,1)S(1)}, bf16[128,256]{1,0:T(8,128)(2,1)}, u32[]{:S(2)}) copy-start(bf16[128,256]{1,0:T(8,128)(2,1)} %param.12) | copy-start | bytes 196612
  10.4 27.7 %all-to-all-start = ((bf16[64,2,256]{2,1,0:T(2,128)(2,1)}), bf16[64,2,256]{2,1,0:T(2,128)(2,1)S(1)}, u32[]{:S(2)}, u32[]{:S(2)}) async-start(bf16[64,2,256]{2,1,0:T(2,128)(2,1)} %all_to_all.55), calls=%async_computation | async-start | bytes 131072 | tf_op jit(solution)/shard_map/all_to_all | solution.py:199
  25.9 3.6 copy-start.4
  26.0 60.2 %collective-permute-start.2 = (bf16[128,6]{1,0:T(8,128)(2,1)S(1)}, bf16[128,6]{1,0:T(8,128)(2,1)S(1)}, u32[]{:S(2)}, u32[]{:S(2)}) collective-permute-start(bf16[128,6]{1,0:T(8,128)(2,1)S(1)} %slice.274), channel_id=1, source_target_pairs={{0,8},{8,16},{16,24},{24,32},{32,40},{40,48},{48,56},{56,64},{64,7... | collective-permute-start | bytes 4616 | tf_op jit(solution)/shard_map/ppermute | solution.py:13
  29.6 2.7 copy-start.6
  29.6 56.6 %collective-permute-start.1 = (bf16[128,6]{1,0:T(8,128)(2,1)S(1)}, bf16[128,6]{1,0:T(8,128)(2,1)S(1)}, u32[]{:S(2)}, u32[]{:S(2)}) collective-permute-start(bf16[128,6]{1,0:T(8,128)(2,1)S(1)} %slice.258), channel_id=1, source_target_pairs={{0,8},{8,16},{16,24},{24,32},{32,40},{40,48},{48,56},{56,64},{64,7... | collective-permute-start | bytes 4616 | tf_op jit(solution)/shard_map/ppermute | solution.py:13
  33.0 0.9 copy-start.2
  33.1 0.7 copy-start.8
  33.8 0.8 copy-start.1
  38.1 21.5 %all-to-all-start.3 = ((bf16[64,2,256]{2,1,0:T(2,128)(2,1)}), bf16[64,2,256]{2,1,0:T(2,128)(2,1)S(1)}, u32[]{:S(2)}, u32[]{:S(2)}) async-start(bf16[64,2,256]{2,1,0:T(2,128)(2,1)} %all_to_all.62), calls=%async_computation.3 | async-start | bytes 131072 | tf_op jit(solution)/shard_map/all_to_all | solution.py:205
  81.3 17.0 %all-to-all-start.4 = ((bf16[2,64,256]{2,0,1:T(2,128)(2,1)}), bf16[2,64,256]{2,0,1:T(2,128)(2,1)S(1)}, u32[]{:S(2)}, u32[]{:S(2)}) async-start(bf16[2,64,256]{2,0,1:T(2,128)(2,1)} %copy.232), calls=%async_computation.4 | async-start | bytes 131072 | tf_op jit(solution)/shard_map/all_to_all | solution.py:210
  98.9 11.8 %collective-permute-start.5 = (bf16[128,6]{1,0:T(8,128)(2,1)S(1)}, bf16[128,6]{1,0:T(8,128)(2,1)S(1)}, u32[]{:S(2)}, u32[]{:S(2)}) collective-permute-start(bf16[128,6]{1,0:T(8,128)(2,1)S(1)} %slice.349), channel_id=1, source_target_pairs={{8,0},{16,8},{24,16},{32,24},{40,32},{48,40},{56,48},{64,56},{72,6... | collective-permute-start | bytes 4616 | tf_op jit(solution)/shard_map/ppermute | solution.py:13
  102.3 18.2 %all-to-all-start.1 = ((bf16[64,2,256]{2,1,0:T(2,128)(2,1)}), bf16[64,2,256]{2,1,0:T(2,128)(2,1)S(1)}, u32[]{:S(2)}, u32[]{:S(2)}) async-start(bf16[64,2,256]{2,1,0:T(2,128)(2,1)} %all_to_all.58), calls=%async_computation.1 | async-start | bytes 131072 | tf_op jit(solution)/shard_map/all_to_all | solution.py:198
  108.3 5.5 collective-permute-start.4
  165.9 19.1 %all-to-all-start.5 = ((bf16[64,2,256]{2,1,0:T(2,128)(2,1)}), bf16[64,2,256]{2,1,0:T(2,128)(2,1)S(1)}, u32[]{:S(2)}, u32[]{:S(2)}) async-start(bf16[64,2,256]{2,1,0:T(2,128)(2,1)} %constant_dynamic-update-slice_fusion), calls=%async_computation.5 | async-start | bytes 131072 | tf_op jit(solution)/shard_map/all_to_all | solution.py:212
  185.1 377.8 %all-to-all-start.2 = ((bf16[2,64,256]{2,0,1:T(2,128)(2,1)}), bf16[2,64,256]{2,0,1:T(2,128)(2,1)S(1)}, u32[]{:S(2)}, u32[]{:S(2)}) async-start(bf16[2,64,256]{2,0,1:T(2,128)(2,1)} %copy.219), calls=%async_computation.2 | async-start | bytes 131072 | tf_op jit(solution)/shard_map/all_to_all | solution.py:204
  563.7 9.3 %collective-permute-start.3 = (bf16[128,6]{1,0:T(8,128)(2,1)S(1)}, bf16[128,6]{1,0:T(8,128)(2,1)S(1)}, u32[]{:S(2)}, u32[]{:S(2)}) collective-permute-start(bf16[128,6]{1,0:T(8,128)(2,1)S(1)} %slice.333), channel_id=1, source_target_pairs={{8,0},{16,8},{24,16},{32,24},{40,32},{48,40},{56,48},{64,56},{72,6... | collective-permute-start | bytes 4616 | tf_op jit(solution)/shard_map/ppermute | solution.py:13
